TPU v7x, 32 devices: a whole 2x2x4 slice. The times are simulated.
32 devices in a mesh: survey: 2 (over y), gz: 4 (over z), gy: 2 (over x), pat: 2 (over core).
Axes of the slice: x: 2, y: 2, z: 4, core: 2. Of those that a mesh axis runs over, the one named last changes fastest.
Arguments:
- conductivity: float32 [32, 256, 512], P(('survey', 'gz'), 'gy'), parts along dimension 0, may hold values from 0.3 to 3
- receivers: int32 [4, 3, 64], P(('survey', 'pat')), parts along dimension 0, may hold values from 0 to 511, as said below
- observed: float32 [4, 64], P(('survey', 'pat')), parts along dimension 0, may hold values from -6 to 6
- potential: float32 [2, 32, 256, 512], P('pat', ('survey', 'gz'), 'gy'), parts along dimension 1, may hold values from -6 to 6
- adjoint_prev: float32 [2, 32, 256, 512], P('pat', ('survey', 'gz'), 'gy'), parts along dimension 1, may hold values from -0.046875 to 0.046875
Outputs:
- adjoint: float32 [2, 32, 256, 512], P('pat', ('survey', 'gz'), 'gy'), parts along dimension 1
- gradient: float32 [32, 256, 512], P(('survey', 'gz'), 'gy'), parts along dimension 0
There are 2 independent parts, one for each index of `survey`. A program takes and returns all parts, laid end to end along the dimension named above; each array names one. Nothing has to cross between parts.
Inputs may be any that keep to these rules, and one draw needn't show every extreme that they name: receivers[p, 0, r], receivers[p, 1, r] and receivers[p, 2, r] are a z cell below 16, a y cell below 256 and an x cell below 512; several receivers may share a cell.
All inputs are finite; a program needn't handle non-finite values.
Results may differ from a plain program's by a relative error of at most 0.0003.
Values sent between devices are 32-bit elements; how exact they have to be, the bound alone decides.
A program may use at most 64 MiB of HBM per device.

v0:
```python
import jax
import jax.numpy as jnp
from jax import lax
from jax.sharding import PartitionSpec as P

relax_weight = 0.8


def extended_2(cells, sides, width):
    for axis, dim in sides:
        count = lax.axis_size(axis)
        ends = count - 1
        head = lax.slice_in_dim(cells, 0, width, axis=dim)
        tail = lax.slice_in_dim(cells, cells.shape[dim] - width, cells.shape[dim], axis=dim)
        cells = jnp.concatenate(
            [
                lax.ppermute(tail, axis, [(i, (i + 1) % count) for i in range(ends)]),
                cells,
                lax.ppermute(head, axis, [((i + 1) % count, i) for i in range(ends)]),
            ],
            axis=dim,
        )
    return cells


def beside_cells(extended):
    widened = jnp.pad(extended, [(0, 0)] * (extended.ndim - 1) + [(1, 1)])
    centre = widened[..., 1:-1, 1:-1, 1:-1]
    others = [
        widened[..., 2:, 1:-1, 1:-1],
        widened[..., :-2, 1:-1, 1:-1],
        widened[..., 1:-1, 2:, 1:-1],
        widened[..., 1:-1, :-2, 1:-1],
        widened[..., 1:-1, 1:-1, 2:],
        widened[..., 1:-1, 1:-1, :-2],
    ]
    return (centre, others)


def relax(cond_ext, adjoint_ext, source):
    cond_mid, cond_near = beside_cells(cond_ext)
    adj_mid, adj_near = beside_cells(adjoint_ext)
    diagonal = jnp.zeros_like(cond_mid)
    coupled = jnp.zeros_like(adj_mid)
    for cond_side, adj_side in zip(cond_near, adj_near):
        face_coef = 0.5 * (cond_mid + cond_side)
        diagonal = diagonal + face_coef
        coupled = coupled + face_coef * adj_side
    updated = adj_mid + relax_weight * (source - diagonal * adj_mid + coupled) / diagonal
    return updated


def contribution(pot_ext, adj_ext):
    pot_mid, pot_near = beside_cells(pot_ext)
    adj_mid, adj_near = beside_cells(adj_ext)
    summed = jnp.zeros_like(adj_mid)
    for pot_side, adj_side in zip(pot_near, adj_near):
        summed = summed + (pot_mid - pot_side) * (adj_mid - adj_side)
    return -0.5 * jnp.sum(summed, axis=0)


def receiver_source(field, receivers, observed, z_start, y_start):
    z_count = field.shape[1]
    y_count = field.shape[2]
    z_local = receivers[:, 0, :] - z_start
    y_local = receivers[:, 1, :] - y_start
    x_local = receivers[:, 2, :]
    inside = (z_local >= 0) & (z_local < z_count) & (y_local >= 0) & (y_local < y_count)
    z_local = jnp.clip(z_local, 0, z_count - 1)
    y_local = jnp.clip(y_local, 0, y_count - 1)
    pattern_ids = jnp.broadcast_to(
        jnp.arange(field.shape[0], dtype=jnp.int32)[:, None], z_local.shape
    )
    values = jnp.where(
        inside, field[pattern_ids, z_local, y_local, x_local] - observed, jnp.zeros_like(observed)
    )
    return jnp.zeros_like(field).at[pattern_ids, z_local, y_local, x_local].add(values)


def local(conductivity, receivers, observed, potential, adjoint_prev):
    pattern_count = potential.shape[0]
    z_cells = conductivity.shape[0]
    y_cells = conductivity.shape[1]
    z_first = lax.axis_index("gz") * z_cells
    y_first = lax.axis_index("gy") * y_cells
    stacked = jnp.concatenate([conductivity[None], adjoint_prev], axis=0)
    extended = extended_2(stacked, (("gz", 1), ("gy", 2)), 1)
    cond_ext = extended[0]
    source = receiver_source(potential, receivers, observed, z_first, y_first)
    adjoint = relax(cond_ext, extended[1:], source)
    rimmed = extended_2(adjoint, (("gz", 1), ("gy", 2)), 1)
    adjoint = relax(cond_ext, rimmed, source)
    both_ext = extended_2(jnp.concatenate([potential, adjoint], axis=0), (("gz", 1), ("gy", 2)), 1)
    partial_grad = contribution(both_ext[:pattern_count], both_ext[pattern_count:])
    gradient = lax.psum(partial_grad, "pat")
    return (adjoint, gradient)


def solution(mesh):
    return jax.shard_map(
        local,
        mesh=mesh,
        in_specs=(
            P(("survey", "gz"), "gy", None),
            P(("survey", "pat"), None, None),
            P(("survey", "pat"), None),
            P("pat", ("survey", "gz"), "gy", None),
            P("pat", ("survey", "gz"), "gy", None),
        ),
        out_specs=(P("pat", ("survey", "gz"), "gy", None), P(("survey", "gz"), "gy", None)),
        check_vma=False,
    )
```

profile of v0, /device:TPU:0, one launch (start us, length us, event | category | flops | bytes accessed | tf_op | source)
XLA Modules:
  0.0 133.2 jit_solution(9145302090978864290)
XLA Ops:
  7.2 0.0 copy-start.2
  7.2 0.0 all-reduce.7.cloned.1.call-start
  7.2 2.4 %pad_maximum_fusion.37 = (f32[2,1,128,512]{3,2,1,0:T(8,128)}, f32[2,1,128,512]{3,2,1,0:T(8,128)}) fusion(f32[1,4,128,512]{3,2,1,0:T(8,128)} %param.9, f32[1,4,128,512]{3,2,1,0:T(8,128)} %bitcast.63), kind=kLoop, calls=%fused_computation.126 | loop fusion | flops 262144 | bytes 3145728 | tf_op jit(solution)/shard_map/slice | solution.py:14
  9.6 5.9 %collective-permute-start = (f32[2,1,128,512]{3,2,1,0:T(8,128)}, f32[2,1,128,512]{3,2,1,0:T(8,128)}, u32[]{:S(2)}, u32[]{:S(2)}) collective-permute-start(f32[2,1,128,512]{3,2,1,0:T(8,128)} %get-tuple-element.12), channel_id=1, source_target_pairs={{0,4},{4,8},{8,12},{1,5},{5,9},{9,13},{2,6},{6,10},{10,14},{3,7},{... | collective-permute-start | bytes 1572872 | tf_op jit(solution)/shard_map/ppermute | solution.py:17
  15.5 1.3 collective-permute-start.1
  16.9 0.0 copy-done.1
  16.9 1.0 gather_fusion
  17.9 8.3 %collective-permute-done = f32[2,1,128,512]{3,2,1,0:T(8,128)} collective-permute-done((f32[2,1,128,512]{3,2,1,0:T(8,128)}, f32[2,1,128,512]{3,2,1,0:T(8,128)}, u32[]{:S(2)}, u32[]{:S(2)}) %collective-permute-start) | collective-permute-done | bytes 524320 | tf_op jit(solution)/shard_map/ppermute | solution.py:17
  26.2 4.9 %collective-permute-done.1 = f32[2,1,128,512]{3,2,1,0:T(8,128)} collective-permute-done((f32[2,1,128,512]{3,2,1,0:T(8,128)}, f32[2,1,128,512]{3,2,1,0:T(8,128)}, u32[]{:S(2)}, u32[]{:S(2)}) %collective-permute-start.1) | collective-permute-done | bytes 524320 | tf_op jit(solution)/shard_map/ppermute | solution.py:19
  31.1 0.0 copy-done.3
  31.1 0.8 pad_maximum_fusion.45
  32.0 3.4 %collective-permute-start.2 = (f32[2,6,1,512]{3,2,1,0:T(1,128)S(1)}, f32[2,6,1,512]{3,2,1,0:T(1,128)S(1)}, u32[]{:S(2)}, u32[]{:S(2)}) collective-permute-start(f32[2,6,1,512]{3,2,1,0:T(1,128)S(1)} %get-tuple-element.8), channel_id=1, source_target_pairs={{0,2},{1,3},{4,6},{5,7},{8,10},{9,11},{12,14},{13,15},{16,18},{17,... | collective-permute-start | bytes 73736 | tf_op jit(solution)/shard_map/ppermute | solution.py:17
  35.4 1.3 collective-permute-start.3
  36.7 1.1 broadcast.273
  37.8 9.4 %scatter_fusion = f32[4,128,512]{2,1,0:T(8,128)} fusion(f32[4,128,512]{2,1,0:T(8,128)} %broadcast.273, s32[64]{0:T(128)S(1)} %get-tuple-element.19, f32[64]{0:T(128)S(1)} %fusion.63), kind=kCustom, calls=%fused_computation.1 | custom fusion | flops 64 | bytes 1536 | tf_op jit(solution)/shard_map/scatter-add | solution.py:77
  47.2 0.0 collective-permute-done.2
  47.2 0.0 collective-permute-done.3
  47.2 1.7 %pad_maximum_fusion = f32[2,6,130,512]{3,2,1,0:T(8,128)S(1)} fusion(f32[2,6,1,512]{3,2,1,0:T(1,128)S(1)} %collective-permute-done.3, f32[2,1,128,512]{3,2,1,0:T(8,128)} %collective-permute-done.1, f32[1,4,128,512]{3,2,1,0:T(8,128)S(1)} %copy-done.2, f32[1,4,128,512]{3,2,1,0:T(8,128)S(1)} %bitcast.65, f32[2,1,128,512]{3,2,1,0:T(8,128)} %collective-permute-done, ...), kind=kLoop, calls=%fused_computation.2 | loop fusion | flops 3993600 | bytes 6389760 | tf_op jit(solution)/shard_map/concatenate | solution.py:15
  48.8 0.0 copy-start.4
  48.9 0.4 slice_bitcast_fusion
  49.2 0.9 copy-done.4
  50.1 4.7 %fusion.11 = f32[1,4,128,512]{3,2,1,0:T(8,128)S(1)} fusion(f32[1,4,128,512]{3,2,1,0:T(8,128)S(1)} %copy-done.2, f32[1,6,130,512]{3,2,1,0:T(8,128)S(1)} %get-tuple-element.5, f32[2,6,1,512]{3,2,1,0:T(1,128)S(1)} %collective-permute-done.2, f32[2,1,128,512]{3,2,1,0:T(8,128)} %collective-permute-done.1, f32[2,1,128,512]{3,2,1,0:T(8,128)} %collective-permute-done, ...), kind=kLoop, calls=%fused_computation.30 | loop fusion | flops 12058624 | bytes 13877248 | tf_op jit(solution)/shard_map/add | solution.py:49
  54.8 2.7 %collective-permute-start.5 = (f32[1,1,128,512]{3,2,1,0:T(8,128)S(1)}, f32[1,1,128,512]{3,2,1,0:T(8,128)S(1)}, u32[]{:S(2)}, u32[]{:S(2)}) collective-permute-start(f32[1,1,128,512]{3,2,1,0:T(8,128)S(1)} %get-tuple-element.16), channel_id=1, source_target_pairs={{0,4},{4,8},{8,12},{1,5},{5,9},{9,13},{2,6},{6,10},{10,14},{3,7},{... | collective-permute-start | bytes 786440 | tf_op jit(solution)/shard_map/ppermute | solution.py:17
  57.5 1.3 collective-permute-start.4
  58.8 2.8 %collective-permute-done.5 = f32[1,1,128,512]{3,2,1,0:T(8,128)S(1)} collective-permute-done((f32[1,1,128,512]{3,2,1,0:T(8,128)S(1)}, f32[1,1,128,512]{3,2,1,0:T(8,128)S(1)}, u32[]{:S(2)}, u32[]{:S(2)}) %collective-permute-start.5) | collective-permute-done | bytes 262176 | tf_op jit(solution)/shard_map/ppermute | solution.py:17
  61.6 4.2 %collective-permute-done.4 = f32[1,1,128,512]{3,2,1,0:T(8,128)S(1)} collective-permute-done((f32[1,1,128,512]{3,2,1,0:T(8,128)S(1)}, f32[1,1,128,512]{3,2,1,0:T(8,128)S(1)}, u32[]{:S(2)}, u32[]{:S(2)}) %collective-permute-start.4) | collective-permute-done | bytes 262176 | tf_op jit(solution)/shard_map/ppermute | solution.py:19
  65.8 4.6 %collective-permute-start.7 = (f32[1,6,1,512]{3,2,1,0:T(1,128)S(1)}, f32[1,6,1,512]{3,2,1,0:T(1,128)S(1)}, u32[]{:S(2)}, u32[]{:S(2)}) collective-permute-start(f32[1,6,1,512]{3,2,1,0:T(1,128)S(1)} %get-tuple-element.14), channel_id=1, source_target_pairs={{0,2},{1,3},{4,6},{5,7},{8,10},{9,11},{12,14},{13,15},{16,18},{17,... | collective-permute-start | bytes 36872 | tf_op jit(solution)/shard_map/ppermute | solution.py:17
  70.3 1.3 collective-permute-start.6
  71.6 0.1 collective-permute-done.7
  71.7 4.2 %collective-permute-done.6 = f32[1,6,1,512]{3,2,1,0:T(1,128)S(1)} collective-permute-done((f32[1,6,1,512]{3,2,1,0:T(1,128)S(1)}, f32[1,6,1,512]{3,2,1,0:T(1,128)S(1)}, u32[]{:S(2)}, u32[]{:S(2)}) %collective-permute-start.6) | collective-permute-done | bytes 12320 | tf_op jit(solution)/shard_map/ppermute | solution.py:19
  75.9 0.7 select_maximum_fusion
  76.7 3.4 %fusion.38 = f32[1,4,128,512]{3,2,1,0:T(8,128)S(1)} fusion(f32[1,4,128,512]{3,2,1,0:T(8,128)S(1)} %fusion.11, f32[1,6,130,514]{3,2,1,0:T(8,128)S(1)} %select_maximum_fusion, f32[1,6,1,512]{3,2,1,0:T(1,128)S(1)} %collective-permute-done.7, f32[1,1,128,512]{3,2,1,0:T(8,128)S(1)} %collective-permute-done.4, f32[1,1,128,512]{3,2,1,0:T(8,128)S(1)} %collective-permute-done.5, ...), kind=kLoop, calls=%fused_computation.74 | loop fusion | flops 11010048 | bytes 12705792 | tf_op jit(solution)/shard_map/add | solution.py:49
  80.1 0.0 copy-start
  80.1 0.1 pad_maximum_fusion.34
  80.2 3.6 %collective-permute-start.9 = (f32[2,1,128,512]{3,2,1,0:T(8,128)S(1)}, f32[2,1,128,512]{3,2,1,0:T(8,128)S(1)}, u32[]{:S(2)}, u32[]{:S(2)}) collective-permute-start(f32[2,1,128,512]{3,2,1,0:T(8,128)S(1)} %get-tuple-element.10), channel_id=1, source_target_pairs={{0,4},{4,8},{8,12},{1,5},{5,9},{9,13},{2,6},{6,10},{10,14},{3,7},{... | collective-permute-start | bytes 1572872 | tf_op jit(solution)/shard_map/ppermute | solution.py:17
  83.8 1.3 collective-permute-start.8
  85.1 5.3 %collective-permute-done.9 = f32[2,1,128,512]{3,2,1,0:T(8,128)S(1)} collective-permute-done((f32[2,1,128,512]{3,2,1,0:T(8,128)S(1)}, f32[2,1,128,512]{3,2,1,0:T(8,128)S(1)}, u32[]{:S(2)}, u32[]{:S(2)}) %collective-permute-start.9) | collective-permute-done | bytes 524320 | tf_op jit(solution)/shard_map/ppermute | solution.py:17
  90.4 4.4 %collective-permute-done.8 = f32[2,1,128,512]{3,2,1,0:T(8,128)S(1)} collective-permute-done((f32[2,1,128,512]{3,2,1,0:T(8,128)S(1)}, f32[2,1,128,512]{3,2,1,0:T(8,128)S(1)}, u32[]{:S(2)}, u32[]{:S(2)}) %collective-permute-start.8) | collective-permute-done | bytes 524320 | tf_op jit(solution)/shard_map/ppermute | solution.py:19
  94.9 1.6 %collective-permute-start.11 = (f32[2,6,1,512]{3,2,1,0:T(1,128)S(1)}, f32[2,6,1,512]{3,2,1,0:T(1,128)S(1)}, u32[]{:S(2)}, u32[]{:S(2)}) collective-permute-start(f32[2,6,1,512]{3,2,1,0:T(1,128)S(1)} %get-tuple-element.6), channel_id=1, source_target_pairs={{0,2},{1,3},{4,6},{5,7},{8,10},{9,11},{12,14},{13,15},{16,18},{17,... | collective-permute-start | bytes 73736 | tf_op jit(solution)/shard_map/ppermute | solution.py:17
  96.6 1.3 collective-permute-start.10
  97.9 0.2 collective-permute-done.11
  98.1 4.2 %collective-permute-done.10 = f32[2,6,1,512]{3,2,1,0:T(1,128)S(1)} collective-permute-done((f32[2,6,1,512]{3,2,1,0:T(1,128)S(1)}, f32[2,6,1,512]{3,2,1,0:T(1,128)S(1)}, u32[]{:S(2)}, u32[]{:S(2)}) %collective-permute-start.10) | collective-permute-done | bytes 24608 | tf_op jit(solution)/shard_map/ppermute | solution.py:19
  102.3 0.4 pad_maximum_fusion.1
  102.7 0.3 fusion.64
  103.1 4.3 %fusion.18 = f32[4,128,512]{2,1,0:T(8,128)} fusion(f32[1,4,128,512]{3,2,1,0:T(8,128)S(1)} %copy-done.1, f32[1,6,130,512]{3,2,1,0:T(8,128)S(1)} %get-tuple-element.3, f32[1,4,128,512]{3,2,1,0:T(8,128)S(1)} %fusion.38, f32[1,6,130,512]{3,2,1,0:T(8,128)S(1)} %get-tuple-element.2, f32[2,6,1,512]{3,2,1,0:T(1,128)S(1)} %collective-permute-done.11, ...), kind=kLoop, calls=%fused_computation.37 | loop fusion | flops 12582912 | bytes 7438336 | tf_op jit(solution)/shard_map/mul | solution.py:59
  107.3 0.0 all-reduce.7.cloned.1.call-update
  107.4 16.7 %all-reduce.7.cloned.1.call-done = f32[4,128,512]{2,1,0:T(8,128)} async-done(((f32[4,128,512]{2,1,0:T(8,128)}), f32[4,128,512]{2,1,0:T(8,128)}) %all-reduce.7.cloned.1.call-update) | async-done | bytes 1048592 | tf_op jit(solution)/shard_map/psum | solution.py:95
  124.1 2.3 %copy.9 = f32[4,128,512]{2,1,0:T(8,128)} copy(f32[4,128,512]{2,1,0:T(8,128)} %all-reduce.7.cloned.1.call-done) | data formatting | bytes 2097152
  (16 shorter events, 0.2 us)
Async XLA Ops:
  7.2 23.9 %copy-start.2 = (f32[1,4,128,512]{3,2,1,0:T(8,128)S(1)}, f32[1,4,128,512]{3,2,1,0:T(8,128)}, u32[]{:S(2)}) copy-start(f32[1,4,128,512]{3,2,1,0:T(8,128)} %param.9) | copy-start | bytes 3145732
  7.2 23.9 %copy-start.3 = (f32[4,128,512]{2,1,0:T(8,128)S(1)}, f32[4,128,512]{2,1,0:T(8,128)}, u32[]{:S(2)}) copy-start(f32[4,128,512]{2,1,0:T(8,128)} %param.5) | copy-start | bytes 3145732
  7.2 9.6 %copy-start.5 = (s32[1,3,64]{2,0,1:T(1,128)S(1)}, s32[1,3,64]{2,0,1:T(1,128)}, u32[]{:S(2)}) copy-start(s32[1,3,64]{2,0,1:T(1,128)} %param.6) | copy-start | bytes 2308
  7.2 9.7 %copy-start.1 = (f32[1,4,128,512]{3,2,1,0:T(8,128)S(1)}, f32[1,4,128,512]{3,2,1,0:T(8,128)}, u32[]{:S(2)}) copy-start(f32[1,4,128,512]{3,2,1,0:T(8,128)} %param.8) | copy-start | bytes 3145732
  7.2 116.9 %all-reduce.7.cloned.1.call-start = ((), (), s32[]{:S(2)}) async-start(), calls=%async_computation | async-start | bytes 2097152 | tf_op jit(solution)/shard_map/psum | solution.py:95
  9.6 27.0 %copy-start.6 = (f32[1,64]{1,0:T(1,128)S(1)}, f32[1,64]{1,0:T(1,128)}, u32[]{:S(2)}) copy-start(f32[1,64]{1,0:T(1,128)} %param.7) | copy-start | bytes 772
  9.6 16.6 %collective-permute-start = (f32[2,1,128,512]{3,2,1,0:T(8,128)}, f32[2,1,128,512]{3,2,1,0:T(8,128)}, u32[]{:S(2)}, u32[]{:S(2)}) collective-permute-start(f32[2,1,128,512]{3,2,1,0:T(8,128)} %get-tuple-element.12), channel_id=1, source_target_pairs={{0,4},{4,8},{8,12},{1,5},{5,9},{9,13},{2,6},{6,10},{10,14},{3,7},{... | collective-permute-start | bytes 1572872 | tf_op jit(solution)/shard_map/ppermute | solution.py:17
  15.5 15.6 %collective-permute-start.1 = (f32[2,1,128,512]{3,2,1,0:T(8,128)}, f32[2,1,128,512]{3,2,1,0:T(8,128)}, u32[]{:S(2)}, u32[]{:S(2)}) collective-permute-start(f32[2,1,128,512]{3,2,1,0:T(8,128)} %get-tuple-element.13), channel_id=1, source_target_pairs={{4,0},{8,4},{12,8},{5,1},{9,5},{13,9},{6,2},{10,6},{14,10},{7,3},{... | collective-permute-start | bytes 1572872 | tf_op jit(solution)/shard_map/ppermute | solution.py:19
  32.0 15.2 %collective-permute-start.2 = (f32[2,6,1,512]{3,2,1,0:T(1,128)S(1)}, f32[2,6,1,512]{3,2,1,0:T(1,128)S(1)}, u32[]{:S(2)}, u32[]{:S(2)}) collective-permute-start(f32[2,6,1,512]{3,2,1,0:T(1,128)S(1)} %get-tuple-element.8), channel_id=1, source_target_pairs={{0,2},{1,3},{4,6},{5,7},{8,10},{9,11},{12,14},{13,15},{16,18},{17,... | collective-permute-start | bytes 73736 | tf_op jit(solution)/shard_map/ppermute | solution.py:17
  35.4 11.8 %collective-permute-start.3 = (f32[2,6,1,512]{3,2,1,0:T(1,128)S(1)}, f32[2,6,1,512]{3,2,1,0:T(1,128)S(1)}, u32[]{:S(2)}, u32[]{:S(2)}) collective-permute-start(f32[2,6,1,512]{3,2,1,0:T(1,128)S(1)} %get-tuple-element.9), channel_id=1, source_target_pairs={{2,0},{3,1},{6,4},{7,5},{10,8},{11,9},{14,12},{15,13},{18,16},{19,... | collective-permute-start | bytes 73736 | tf_op jit(solution)/shard_map/ppermute | solution.py:19
  48.8 1.2 copy-start.4
  54.8 6.8 %collective-permute-start.5 = (f32[1,1,128,512]{3,2,1,0:T(8,128)S(1)}, f32[1,1,128,512]{3,2,1,0:T(8,128)S(1)}, u32[]{:S(2)}, u32[]{:S(2)}) collective-permute-start(f32[1,1,128,512]{3,2,1,0:T(8,128)S(1)} %get-tuple-element.16), channel_id=1, source_target_pairs={{0,4},{4,8},{8,12},{1,5},{5,9},{9,13},{2,6},{6,10},{10,14},{3,7},{... | collective-permute-start | bytes 786440 | tf_op jit(solution)/shard_map/ppermute | solution.py:17
  57.5 8.3 %collective-permute-start.4 = (f32[1,1,128,512]{3,2,1,0:T(8,128)S(1)}, f32[1,1,128,512]{3,2,1,0:T(8,128)S(1)}, u32[]{:S(2)}, u32[]{:S(2)}) collective-permute-start(f32[1,1,128,512]{3,2,1,0:T(8,128)S(1)} %get-tuple-element.17), channel_id=1, source_target_pairs={{4,0},{8,4},{12,8},{5,1},{9,5},{13,9},{6,2},{10,6},{14,10},{7,3},{... | collective-permute-start | bytes 786440 | tf_op jit(solution)/shard_map/ppermute | solution.py:19
  65.8 6.0 %collective-permute-start.7 = (f32[1,6,1,512]{3,2,1,0:T(1,128)S(1)}, f32[1,6,1,512]{3,2,1,0:T(1,128)S(1)}, u32[]{:S(2)}, u32[]{:S(2)}) collective-permute-start(f32[1,6,1,512]{3,2,1,0:T(1,128)S(1)} %get-tuple-element.14), channel_id=1, source_target_pairs={{0,2},{1,3},{4,6},{5,7},{8,10},{9,11},{12,14},{13,15},{16,18},{17,... | collective-permute-start | bytes 36872 | tf_op jit(solution)/shard_map/ppermute | solution.py:17
  70.3 5.6 %collective-permute-start.6 = (f32[1,6,1,512]{3,2,1,0:T(1,128)S(1)}, f32[1,6,1,512]{3,2,1,0:T(1,128)S(1)}, u32[]{:S(2)}, u32[]{:S(2)}) collective-permute-start(f32[1,6,1,512]{3,2,1,0:T(1,128)S(1)} %get-tuple-element.15), channel_id=1, source_target_pairs={{2,0},{3,1},{6,4},{7,5},{10,8},{11,9},{14,12},{15,13},{18,16},{19,... | collective-permute-start | bytes 36872 | tf_op jit(solution)/shard_map/ppermute | solution.py:19
  80.1 23.0 %copy-start = (f32[1,4,128,512]{3,2,1,0:T(8,128)}, f32[1,4,128,512]{3,2,1,0:T(8,128)S(1)}, u32[]{:S(2)}) copy-start(f32[1,4,128,512]{3,2,1,0:T(8,128)S(1)} %fusion.38) | copy-start | bytes 3145732
  80.2 10.2 %collective-permute-start.9 = (f32[2,1,128,512]{3,2,1,0:T(8,128)S(1)}, f32[2,1,128,512]{3,2,1,0:T(8,128)S(1)}, u32[]{:S(2)}, u32[]{:S(2)}) collective-permute-start(f32[2,1,128,512]{3,2,1,0:T(8,128)S(1)} %get-tuple-element.10), channel_id=1, source_target_pairs={{0,4},{4,8},{8,12},{1,5},{5,9},{9,13},{2,6},{6,10},{10,14},{3,7},{... | collective-permute-start | bytes 1572872 | tf_op jit(solution)/shard_map/ppermute | solution.py:17
  83.8 11.1 %collective-permute-start.8 = (f32[2,1,128,512]{3,2,1,0:T(8,128)S(1)}, f32[2,1,128,512]{3,2,1,0:T(8,128)S(1)}, u32[]{:S(2)}, u32[]{:S(2)}) collective-permute-start(f32[2,1,128,512]{3,2,1,0:T(8,128)S(1)} %get-tuple-element.11), channel_id=1, source_target_pairs={{4,0},{8,4},{12,8},{5,1},{9,5},{13,9},{6,2},{10,6},{14,10},{7,3},{... | collective-permute-start | bytes 1572872 | tf_op jit(solution)/shard_map/ppermute | solution.py:19
  94.9 3.2 %collective-permute-start.11 = (f32[2,6,1,512]{3,2,1,0:T(1,128)S(1)}, f32[2,6,1,512]{3,2,1,0:T(1,128)S(1)}, u32[]{:S(2)}, u32[]{:S(2)}) collective-permute-start(f32[2,6,1,512]{3,2,1,0:T(1,128)S(1)} %get-tuple-element.6), channel_id=1, source_target_pairs={{0,2},{1,3},{4,6},{5,7},{8,10},{9,11},{12,14},{13,15},{16,18},{17,... | collective-permute-start | bytes 73736 | tf_op jit(solution)/shard_map/ppermute | solution.py:17
  96.6 5.7 %collective-permute-start.10 = (f32[2,6,1,512]{3,2,1,0:T(1,128)S(1)}, f32[2,6,1,512]{3,2,1,0:T(1,128)S(1)}, u32[]{:S(2)}, u32[]{:S(2)}) collective-permute-start(f32[2,6,1,512]{3,2,1,0:T(1,128)S(1)} %get-tuple-element.7), channel_id=1, source_target_pairs={{2,0},{3,1},{6,4},{7,5},{10,8},{11,9},{14,12},{15,13},{18,16},{19,... | collective-permute-start | bytes 73736 | tf_op jit(solution)/shard_map/ppermute | solution.py:19
Sparse Core Ops, SparseCore 0:
  107.5 16.5 all-reduce.6
where the time goes:
time: 134 us; the launch traced here: 133 us
  waiting for transfers between devices  55.4 us (41%)
  starting transfers between devices  29.5 us (22%)
  other arithmetic  28 us (21%)
  between operations  14.3 us (11%)
  local copies, waits for them, and re-layouts  5.99 us (4%)
    ppermute x6, waiting for transfers between devices, extended_2(): lax.ppermute(head, axis, [((i + 1) % count, i) for i in range(ends)])  21.9 us
    ppermute x6, starting transfers between devices, extended_2(): lax.ppermute(tail, axis, [(i, (i + 1) % count) for i in range(ends)])  21.7 us
    ppermute x6, waiting for transfers between devices, extended_2(): lax.ppermute(tail, axis, [(i, (i + 1) % count) for i in range(ends)])  16.7 us
    psum x1, waiting for transfers between devices, local(): gradient = lax.psum(partial_grad, 'pat')  16.7 us
    scatter-add x1, other arithmetic, receiver_source(): jnp.zeros_like(field).at[pattern_ids, z_local, y_local, x_local].add(values)  9.4 us
    add x2, other arithmetic, relax(): adj_mid + relax_weight * (source - diagonal * adj_mid + coupled) / diagonal  8.09 us
    ppermute x6, starting transfers between devices, extended_2(): lax.ppermute(head, axis, [((i + 1) % count, i) for i in range(ends)])  7.74 us
    mul x1, other arithmetic, contribution(): return -0.5 * jnp.sum(summed, axis=0)  4.25 us
  transfers between devices with their start and end apart: 13, of which 11 were waited for; matrix products, arithmetic and copies ran while one was open for 9% of the time, Pallas kernels for 0%

commit v1 on v0

--- a/solution.py
+++ b/solution.py
@@ -92,7 +92,7 @@
     adjoint = relax(cond_ext, rimmed, source)
     both_ext = extended_2(jnp.concatenate([potential, adjoint], axis=0), (("gz", 1), ("gy", 2)), 1)
     partial_grad = contribution(both_ext[:pattern_count], both_ext[pattern_count:])
-    gradient = lax.psum(partial_grad, "pat")
+    gradient = jnp.sum(lax.all_gather(partial_grad, "pat"), axis=0)
     return (adjoint, gradient)
 
 

time: 134 us -> 126 us (0.940)
  waiting for transfers between devices: 55.4 us -> 46.6 us
  other arithmetic: 28 us -> 30.9 us
  local copies, waits for them, and re-layouts: 5.99 us -> 3.73 us
    psum x1 -> x0, waiting for transfers between devices: 16.7 us -> none  [local(): gradient = lax.psum(partial_grad, 'pat')]
    all_gather x0 -> x1, waiting for transfers between devices: none -> 7.9 us  [local(): gradient = jnp.sum(lax.all_gather(partial_grad, 'pat'), axis=0)]
    reduce_sum x0 -> x1, other arithmetic: none -> 2.87 us  [local(): gradient = jnp.sum(lax.all_gather(partial_grad, 'pat'), axis=0)]
    unnamed x15 -> x14, local copies, waits for them, and re-layouts: 3.15 us -> 0.89 us
where the time goes in v1:
time: 126 us; the launch traced here: 125 us
  waiting for transfers between devices  46.6 us (37%)
  other arithmetic  30.9 us (25%)
  starting transfers between devices  29.5 us (23%)
  between operations  14.3 us (11%)
  local copies, waits for them, and re-layouts  3.73 us (3%)
    ppermute x6, waiting for transfers between devices, extended_2(): lax.ppermute(head, axis, [((i + 1) % count, i) for i in range(ends)])  21.9 us
    ppermute x6, starting transfers between devices, extended_2(): lax.ppermute(tail, axis, [(i, (i + 1) % count) for i in range(ends)])  21.7 us
    ppermute x6, waiting for transfers between devices, extended_2(): lax.ppermute(tail, axis, [(i, (i + 1) % count) for i in range(ends)])  16.7 us
    scatter-add x1, other arithmetic, receiver_source(): jnp.zeros_like(field).at[pattern_ids, z_local, y_local, x_local].add(values)  9.4 us
    add x2, other arithmetic, relax(): adj_mid + relax_weight * (source - diagonal * adj_mid + coupled) / diagonal  8.09 us
    all_gather x1, waiting for transfers between devices, local(): gradient = jnp.sum(lax.all_gather(partial_grad, 'pat'), axis=0)  7.9 us
    ppermute x6, starting transfers between devices, extended_2(): lax.ppermute(head, axis, [((i + 1) % count, i) for i in range(ends)])  7.74 us
    mul x1, other arithmetic, contribution(): return -0.5 * jnp.sum(summed, axis=0)  4.35 us
  transfers between devices with their start and end apart: 13, of which 11 were waited for; matrix products, arithmetic and copies ran while one was open for 9% of the time, Pallas kernels for 0%

profile of v1, /device:TPU:0, one launch (start us, length us, event | category | flops | bytes accessed | tf_op | source)
XLA Modules:
  0.0 125.1 jit_solution(14226037504741916804)
XLA Ops:
  7.2 0.0 copy-start.2
  7.2 0.0 all-gather.2.cloned.1.call-start
  7.2 2.4 %pad_maximum_fusion.37 = (f32[2,1,128,512]{3,2,1,0:T(8,128)}, f32[2,1,128,512]{3,2,1,0:T(8,128)}) fusion(f32[1,4,128,512]{3,2,1,0:T(8,128)} %param.9, f32[1,4,128,512]{3,2,1,0:T(8,128)} %bitcast.61), kind=kLoop, calls=%fused_computation.125 | loop fusion | flops 262144 | bytes 3145728 | tf_op jit(solution)/shard_map/slice | solution.py:14
  9.6 5.9 %collective-permute-start = (f32[2,1,128,512]{3,2,1,0:T(8,128)}, f32[2,1,128,512]{3,2,1,0:T(8,128)}, u32[]{:S(2)}, u32[]{:S(2)}) collective-permute-start(f32[2,1,128,512]{3,2,1,0:T(8,128)} %get-tuple-element.12), channel_id=1, source_target_pairs={{0,4},{4,8},{8,12},{1,5},{5,9},{9,13},{2,6},{6,10},{10,14},{3,7},{... | collective-permute-start | bytes 1572872 | tf_op jit(solution)/shard_map/ppermute | solution.py:17
  15.5 1.3 %collective-permute-start.1 = (f32[2,1,128,512]{3,2,1,0:T(8,128)}, f32[2,1,128,512]{3,2,1,0:T(8,128)}, u32[]{:S(2)}, u32[]{:S(2)}) collective-permute-start(f32[2,1,128,512]{3,2,1,0:T(8,128)} %get-tuple-element.13), channel_id=1, source_target_pairs={{4,0},{8,4},{12,8},{5,1},{9,5},{13,9},{6,2},{10,6},{14,10},{7,3},{... | collective-permute-start | bytes 1572872 | tf_op jit(solution)/shard_map/ppermute | solution.py:19
  16.9 0.0 copy-done.1
  16.9 1.0 gather_fusion
  17.9 8.3 %collective-permute-done = f32[2,1,128,512]{3,2,1,0:T(8,128)} collective-permute-done((f32[2,1,128,512]{3,2,1,0:T(8,128)}, f32[2,1,128,512]{3,2,1,0:T(8,128)}, u32[]{:S(2)}, u32[]{:S(2)}) %collective-permute-start) | collective-permute-done | bytes 524320 | tf_op jit(solution)/shard_map/ppermute | solution.py:17
  26.2 4.9 %collective-permute-done.1 = f32[2,1,128,512]{3,2,1,0:T(8,128)} collective-permute-done((f32[2,1,128,512]{3,2,1,0:T(8,128)}, f32[2,1,128,512]{3,2,1,0:T(8,128)}, u32[]{:S(2)}, u32[]{:S(2)}) %collective-permute-start.1) | collective-permute-done | bytes 524320 | tf_op jit(solution)/shard_map/ppermute | solution.py:19
  31.1 0.0 copy-done.3
  31.1 0.8 pad_maximum_fusion.45
  32.0 3.4 %collective-permute-start.2 = (f32[2,6,1,512]{3,2,1,0:T(1,128)S(1)}, f32[2,6,1,512]{3,2,1,0:T(1,128)S(1)}, u32[]{:S(2)}, u32[]{:S(2)}) collective-permute-start(f32[2,6,1,512]{3,2,1,0:T(1,128)S(1)} %get-tuple-element.8), channel_id=1, source_target_pairs={{0,2},{1,3},{4,6},{5,7},{8,10},{9,11},{12,14},{13,15},{16,18},{17,... | collective-permute-start | bytes 73736 | tf_op jit(solution)/shard_map/ppermute | solution.py:17
  35.4 1.3 %collective-permute-start.3 = (f32[2,6,1,512]{3,2,1,0:T(1,128)S(1)}, f32[2,6,1,512]{3,2,1,0:T(1,128)S(1)}, u32[]{:S(2)}, u32[]{:S(2)}) collective-permute-start(f32[2,6,1,512]{3,2,1,0:T(1,128)S(1)} %get-tuple-element.9), channel_id=1, source_target_pairs={{2,0},{3,1},{6,4},{7,5},{10,8},{11,9},{14,12},{15,13},{18,16},{19,... | collective-permute-start | bytes 73736 | tf_op jit(solution)/shard_map/ppermute | solution.py:19
  36.7 1.1 broadcast.272
  37.8 9.4 %scatter_fusion = f32[4,128,512]{2,1,0:T(8,128)} fusion(f32[4,128,512]{2,1,0:T(8,128)} %broadcast.272, s32[64]{0:T(128)S(1)} %get-tuple-element.19, f32[64]{0:T(128)S(1)} %fusion.62), kind=kCustom, calls=%fused_computation.1 | custom fusion | flops 64 | bytes 1536 | tf_op jit(solution)/shard_map/scatter-add | solution.py:77
  47.2 0.0 collective-permute-done.2
  47.2 0.0 collective-permute-done.3
  47.2 1.7 %pad_maximum_fusion = f32[2,6,130,512]{3,2,1,0:T(8,128)S(1)} fusion(f32[2,6,1,512]{3,2,1,0:T(1,128)S(1)} %collective-permute-done.3, f32[2,1,128,512]{3,2,1,0:T(8,128)} %collective-permute-done.1, f32[1,4,128,512]{3,2,1,0:T(8,128)S(1)} %copy-done.2, f32[1,4,128,512]{3,2,1,0:T(8,128)S(1)} %bitcast.63, f32[2,1,128,512]{3,2,1,0:T(8,128)} %collective-permute-done, ...), kind=kLoop, calls=%fused_computation.2 | loop fusion | flops 3993600 | bytes 6389760 | tf_op jit(solution)/shard_map/concatenate | solution.py:15
  48.8 0.0 copy-start.4
  48.9 0.4 slice_bitcast_fusion
  49.2 0.9 copy-done.4
  50.1 4.7 %fusion.11 = f32[1,4,128,512]{3,2,1,0:T(8,128)S(1)} fusion(f32[1,4,128,512]{3,2,1,0:T(8,128)S(1)} %copy-done.2, f32[1,6,130,512]{3,2,1,0:T(8,128)S(1)} %get-tuple-element.5, f32[2,6,1,512]{3,2,1,0:T(1,128)S(1)} %collective-permute-done.2, f32[2,1,128,512]{3,2,1,0:T(8,128)} %collective-permute-done.1, f32[2,1,128,512]{3,2,1,0:T(8,128)} %collective-permute-done, ...), kind=kLoop, calls=%fused_computation.30 | loop fusion | flops 12058624 | bytes 13877248 | tf_op jit(solution)/shard_map/add | solution.py:49
  54.8 2.7 %collective-permute-start.5 = (f32[1,1,128,512]{3,2,1,0:T(8,128)S(1)}, f32[1,1,128,512]{3,2,1,0:T(8,128)S(1)}, u32[]{:S(2)}, u32[]{:S(2)}) collective-permute-start(f32[1,1,128,512]{3,2,1,0:T(8,128)S(1)} %get-tuple-element.16), channel_id=1, source_target_pairs={{0,4},{4,8},{8,12},{1,5},{5,9},{9,13},{2,6},{6,10},{10,14},{3,7},{... | collective-permute-start | bytes 786440 | tf_op jit(solution)/shard_map/ppermute | solution.py:17
  57.5 1.3 %collective-permute-start.4 = (f32[1,1,128,512]{3,2,1,0:T(8,128)S(1)}, f32[1,1,128,512]{3,2,1,0:T(8,128)S(1)}, u32[]{:S(2)}, u32[]{:S(2)}) collective-permute-start(f32[1,1,128,512]{3,2,1,0:T(8,128)S(1)} %get-tuple-element.17), channel_id=1, source_target_pairs={{4,0},{8,4},{12,8},{5,1},{9,5},{13,9},{6,2},{10,6},{14,10},{7,3},{... | collective-permute-start | bytes 786440 | tf_op jit(solution)/shard_map/ppermute | solution.py:19
  58.8 2.8 %collective-permute-done.5 = f32[1,1,128,512]{3,2,1,0:T(8,128)S(1)} collective-permute-done((f32[1,1,128,512]{3,2,1,0:T(8,128)S(1)}, f32[1,1,128,512]{3,2,1,0:T(8,128)S(1)}, u32[]{:S(2)}, u32[]{:S(2)}) %collective-permute-start.5) | collective-permute-done | bytes 262176 | tf_op jit(solution)/shard_map/ppermute | solution.py:17
  61.6 4.2 %collective-permute-done.4 = f32[1,1,128,512]{3,2,1,0:T(8,128)S(1)} collective-permute-done((f32[1,1,128,512]{3,2,1,0:T(8,128)S(1)}, f32[1,1,128,512]{3,2,1,0:T(8,128)S(1)}, u32[]{:S(2)}, u32[]{:S(2)}) %collective-permute-start.4) | collective-permute-done | bytes 262176 | tf_op jit(solution)/shard_map/ppermute | solution.py:19
  65.8 4.6 %collective-permute-start.7 = (f32[1,6,1,512]{3,2,1,0:T(1,128)S(1)}, f32[1,6,1,512]{3,2,1,0:T(1,128)S(1)}, u32[]{:S(2)}, u32[]{:S(2)}) collective-permute-start(f32[1,6,1,512]{3,2,1,0:T(1,128)S(1)} %get-tuple-element.14), channel_id=1, source_target_pairs={{0,2},{1,3},{4,6},{5,7},{8,10},{9,11},{12,14},{13,15},{16,18},{17,... | collective-permute-start | bytes 36872 | tf_op jit(solution)/shard_map/ppermute | solution.py:17
  70.3 1.3 %collective-permute-start.6 = (f32[1,6,1,512]{3,2,1,0:T(1,128)S(1)}, f32[1,6,1,512]{3,2,1,0:T(1,128)S(1)}, u32[]{:S(2)}, u32[]{:S(2)}) collective-permute-start(f32[1,6,1,512]{3,2,1,0:T(1,128)S(1)} %get-tuple-element.15), channel_id=1, source_target_pairs={{2,0},{3,1},{6,4},{7,5},{10,8},{11,9},{14,12},{15,13},{18,16},{19,... | collective-permute-start | bytes 36872 | tf_op jit(solution)/shard_map/ppermute | solution.py:19
  71.6 0.1 collective-permute-done.7
  71.7 4.2 %collective-permute-done.6 = f32[1,6,1,512]{3,2,1,0:T(1,128)S(1)} collective-permute-done((f32[1,6,1,512]{3,2,1,0:T(1,128)S(1)}, f32[1,6,1,512]{3,2,1,0:T(1,128)S(1)}, u32[]{:S(2)}, u32[]{:S(2)}) %collective-permute-start.6) | collective-permute-done | bytes 12320 | tf_op jit(solution)/shard_map/ppermute | solution.py:19
  75.9 0.7 select_maximum_fusion
  76.7 3.4 %fusion.37 = f32[1,4,128,512]{3,2,1,0:T(8,128)S(1)} fusion(f32[1,4,128,512]{3,2,1,0:T(8,128)S(1)} %fusion.11, f32[1,6,130,514]{3,2,1,0:T(8,128)S(1)} %select_maximum_fusion, f32[1,6,1,512]{3,2,1,0:T(1,128)S(1)} %collective-permute-done.7, f32[1,1,128,512]{3,2,1,0:T(8,128)S(1)} %collective-permute-done.4, f32[1,1,128,512]{3,2,1,0:T(8,128)S(1)} %collective-permute-done.5, ...), kind=kLoop, calls=%fused_computation.73 | loop fusion | flops 11010048 | bytes 12705792 | tf_op jit(solution)/shard_map/add | solution.py:49
  80.1 0.0 copy-start
  80.1 0.1 pad_maximum_fusion.34
  80.2 3.6 %collective-permute-start.9 = (f32[2,1,128,512]{3,2,1,0:T(8,128)S(1)}, f32[2,1,128,512]{3,2,1,0:T(8,128)S(1)}, u32[]{:S(2)}, u32[]{:S(2)}) collective-permute-start(f32[2,1,128,512]{3,2,1,0:T(8,128)S(1)} %get-tuple-element.10), channel_id=1, source_target_pairs={{0,4},{4,8},{8,12},{1,5},{5,9},{9,13},{2,6},{6,10},{10,14},{3,7},{... | collective-permute-start | bytes 1572872 | tf_op jit(solution)/shard_map/ppermute | solution.py:17
  83.8 1.3 %collective-permute-start.8 = (f32[2,1,128,512]{3,2,1,0:T(8,128)S(1)}, f32[2,1,128,512]{3,2,1,0:T(8,128)S(1)}, u32[]{:S(2)}, u32[]{:S(2)}) collective-permute-start(f32[2,1,128,512]{3,2,1,0:T(8,128)S(1)} %get-tuple-element.11), channel_id=1, source_target_pairs={{4,0},{8,4},{12,8},{5,1},{9,5},{13,9},{6,2},{10,6},{14,10},{7,3},{... | collective-permute-start | bytes 1572872 | tf_op jit(solution)/shard_map/ppermute | solution.py:19
  85.1 5.3 %collective-permute-done.9 = f32[2,1,128,512]{3,2,1,0:T(8,128)S(1)} collective-permute-done((f32[2,1,128,512]{3,2,1,0:T(8,128)S(1)}, f32[2,1,128,512]{3,2,1,0:T(8,128)S(1)}, u32[]{:S(2)}, u32[]{:S(2)}) %collective-permute-start.9) | collective-permute-done | bytes 524320 | tf_op jit(solution)/shard_map/ppermute | solution.py:17
  90.4 4.4 %collective-permute-done.8 = f32[2,1,128,512]{3,2,1,0:T(8,128)S(1)} collective-permute-done((f32[2,1,128,512]{3,2,1,0:T(8,128)S(1)}, f32[2,1,128,512]{3,2,1,0:T(8,128)S(1)}, u32[]{:S(2)}, u32[]{:S(2)}) %collective-permute-start.8) | collective-permute-done | bytes 524320 | tf_op jit(solution)/shard_map/ppermute | solution.py:19
  94.9 1.6 %collective-permute-start.11 = (f32[2,6,1,512]{3,2,1,0:T(1,128)S(1)}, f32[2,6,1,512]{3,2,1,0:T(1,128)S(1)}, u32[]{:S(2)}, u32[]{:S(2)}) collective-permute-start(f32[2,6,1,512]{3,2,1,0:T(1,128)S(1)} %get-tuple-element.6), channel_id=1, source_target_pairs={{0,2},{1,3},{4,6},{5,7},{8,10},{9,11},{12,14},{13,15},{16,18},{17,... | collective-permute-start | bytes 73736 | tf_op jit(solution)/shard_map/ppermute | solution.py:17
  96.6 1.3 %collective-permute-start.10 = (f32[2,6,1,512]{3,2,1,0:T(1,128)S(1)}, f32[2,6,1,512]{3,2,1,0:T(1,128)S(1)}, u32[]{:S(2)}, u32[]{:S(2)}) collective-permute-start(f32[2,6,1,512]{3,2,1,0:T(1,128)S(1)} %get-tuple-element.7), channel_id=1, source_target_pairs={{2,0},{3,1},{6,4},{7,5},{10,8},{11,9},{14,12},{15,13},{18,16},{19,... | collective-permute-start | bytes 73736 | tf_op jit(solution)/shard_map/ppermute | solution.py:19
  97.9 0.2 collective-permute-done.11
  98.1 4.2 %collective-permute-done.10 = f32[2,6,1,512]{3,2,1,0:T(1,128)S(1)} collective-permute-done((f32[2,6,1,512]{3,2,1,0:T(1,128)S(1)}, f32[2,6,1,512]{3,2,1,0:T(1,128)S(1)}, u32[]{:S(2)}, u32[]{:S(2)}) %collective-permute-start.10) | collective-permute-done | bytes 24608 | tf_op jit(solution)/shard_map/ppermute | solution.py:19
  102.3 0.5 pad_maximum_fusion.1
  102.7 0.3 fusion.63
  103.1 4.4 %fusion.17 = f32[1,4,128,512]{3,2,1,0:T(8,128)} fusion(f32[1,4,128,512]{3,2,1,0:T(8,128)S(1)} %copy-done.1, f32[1,6,130,512]{3,2,1,0:T(8,128)S(1)} %get-tuple-element.3, f32[1,4,128,512]{3,2,1,0:T(8,128)S(1)} %fusion.37, f32[1,6,130,512]{3,2,1,0:T(8,128)S(1)} %get-tuple-element.2, f32[2,6,1,512]{3,2,1,0:T(1,128)S(1)} %collective-permute-done.11, ...), kind=kLoop, calls=%fused_computation.36 | loop fusion | flops 12582912 | bytes 7438336 | tf_op jit(solution)/shard_map/mul | solution.py:59
  107.4 0.0 all-gather.2.cloned.1.call-update
  107.5 7.9 %all-gather.2.cloned.1.call-done = f32[2,4,128,512]{3,2,1,0:T(8,128)} async-done(((f32[1,4,128,512]{3,2,1,0:T(8,128)}), f32[2,4,128,512]{3,2,1,0:T(8,128)}) %all-gather.2.cloned.1.call-update) | async-done | bytes 2097168 | tf_op jit(solution)/shard_map/all_gather | solution.py:95
  115.4 2.9 %reduce_sum.8 = f32[4,128,512]{2,1,0:T(8,128)} reduce(f32[2,4,128,512]{3,2,1,0:T(8,128)} %all-gather.2.cloned.1.call-done, f32[]{:T(128)} %constant.13.clone.1), dimensions={0}, to_apply=%region_1.2 | reduce | flops 262144 | bytes 3145732 | tf_op jit(solution)/shard_map/reduce_sum | solution.py:95
  (16 shorter events, 0.2 us)
Async XLA Ops:
  7.2 23.9 %copy-start.2 = (f32[1,4,128,512]{3,2,1,0:T(8,128)S(1)}, f32[1,4,128,512]{3,2,1,0:T(8,128)}, u32[]{:S(2)}) copy-start(f32[1,4,128,512]{3,2,1,0:T(8,128)} %param.9) | copy-start | bytes 3145732
  7.2 23.9 %copy-start.3 = (f32[4,128,512]{2,1,0:T(8,128)S(1)}, f32[4,128,512]{2,1,0:T(8,128)}, u32[]{:S(2)}) copy-start(f32[4,128,512]{2,1,0:T(8,128)} %param.5) | copy-start | bytes 3145732
  7.2 9.6 %copy-start.5 = (s32[1,3,64]{2,0,1:T(1,128)S(1)}, s32[1,3,64]{2,0,1:T(1,128)}, u32[]{:S(2)}) copy-start(s32[1,3,64]{2,0,1:T(1,128)} %param.6) | copy-start | bytes 2308
  7.2 9.7 %copy-start.1 = (f32[1,4,128,512]{3,2,1,0:T(8,128)S(1)}, f32[1,4,128,512]{3,2,1,0:T(8,128)}, u32[]{:S(2)}) copy-start(f32[1,4,128,512]{3,2,1,0:T(8,128)} %param.8) | copy-start | bytes 3145732
  7.2 108.2 %all-gather.2.cloned.1.call-start = ((), (), s32[]{:S(2)}) async-start(), calls=%async_computation | async-start | bytes 3145728 | tf_op jit(solution)/shard_map/all_gather | solution.py:95
  9.6 27.0 %copy-start.6 = (f32[1,64]{1,0:T(1,128)S(1)}, f32[1,64]{1,0:T(1,128)}, u32[]{:S(2)}) copy-start(f32[1,64]{1,0:T(1,128)} %param.7) | copy-start | bytes 772
  9.6 16.6 %collective-permute-start = (f32[2,1,128,512]{3,2,1,0:T(8,128)}, f32[2,1,128,512]{3,2,1,0:T(8,128)}, u32[]{:S(2)}, u32[]{:S(2)}) collective-permute-start(f32[2,1,128,512]{3,2,1,0:T(8,128)} %get-tuple-element.12), channel_id=1, source_target_pairs={{0,4},{4,8},{8,12},{1,5},{5,9},{9,13},{2,6},{6,10},{10,14},{3,7},{... | collective-permute-start | bytes 1572872 | tf_op jit(solution)/shard_map/ppermute | solution.py:17
  15.5 15.6 %collective-permute-start.1 = (f32[2,1,128,512]{3,2,1,0:T(8,128)}, f32[2,1,128,512]{3,2,1,0:T(8,128)}, u32[]{:S(2)}, u32[]{:S(2)}) collective-permute-start(f32[2,1,128,512]{3,2,1,0:T(8,128)} %get-tuple-element.13), channel_id=1, source_target_pairs={{4,0},{8,4},{12,8},{5,1},{9,5},{13,9},{6,2},{10,6},{14,10},{7,3},{... | collective-permute-start | bytes 1572872 | tf_op jit(solution)/shard_map/ppermute | solution.py:19
  32.0 15.2 %collective-permute-start.2 = (f32[2,6,1,512]{3,2,1,0:T(1,128)S(1)}, f32[2,6,1,512]{3,2,1,0:T(1,128)S(1)}, u32[]{:S(2)}, u32[]{:S(2)}) collective-permute-start(f32[2,6,1,512]{3,2,1,0:T(1,128)S(1)} %get-tuple-element.8), channel_id=1, source_target_pairs={{0,2},{1,3},{4,6},{5,7},{8,10},{9,11},{12,14},{13,15},{16,18},{17,... | collective-permute-start | bytes 73736 | tf_op jit(solution)/shard_map/ppermute | solution.py:17
  35.4 11.8 %collective-permute-start.3 = (f32[2,6,1,512]{3,2,1,0:T(1,128)S(1)}, f32[2,6,1,512]{3,2,1,0:T(1,128)S(1)}, u32[]{:S(2)}, u32[]{:S(2)}) collective-permute-start(f32[2,6,1,512]{3,2,1,0:T(1,128)S(1)} %get-tuple-element.9), channel_id=1, source_target_pairs={{2,0},{3,1},{6,4},{7,5},{10,8},{11,9},{14,12},{15,13},{18,16},{19,... | collective-permute-start | bytes 73736 | tf_op jit(solution)/shard_map/ppermute | solution.py:19
  48.8 1.2 copy-start.4
  54.8 6.8 %collective-permute-start.5 = (f32[1,1,128,512]{3,2,1,0:T(8,128)S(1)}, f32[1,1,128,512]{3,2,1,0:T(8,128)S(1)}, u32[]{:S(2)}, u32[]{:S(2)}) collective-permute-start(f32[1,1,128,512]{3,2,1,0:T(8,128)S(1)} %get-tuple-element.16), channel_id=1, source_target_pairs={{0,4},{4,8},{8,12},{1,5},{5,9},{9,13},{2,6},{6,10},{10,14},{3,7},{... | collective-permute-start | bytes 786440 | tf_op jit(solution)/shard_map/ppermute | solution.py:17
  57.5 8.3 %collective-permute-start.4 = (f32[1,1,128,512]{3,2,1,0:T(8,128)S(1)}, f32[1,1,128,512]{3,2,1,0:T(8,128)S(1)}, u32[]{:S(2)}, u32[]{:S(2)}) collective-permute-start(f32[1,1,128,512]{3,2,1,0:T(8,128)S(1)} %get-tuple-element.17), channel_id=1, source_target_pairs={{4,0},{8,4},{12,8},{5,1},{9,5},{13,9},{6,2},{10,6},{14,10},{7,3},{... | collective-permute-start | bytes 786440 | tf_op jit(solution)/shard_map/ppermute | solution.py:19
  65.8 6.0 %collective-permute-start.7 = (f32[1,6,1,512]{3,2,1,0:T(1,128)S(1)}, f32[1,6,1,512]{3,2,1,0:T(1,128)S(1)}, u32[]{:S(2)}, u32[]{:S(2)}) collective-permute-start(f32[1,6,1,512]{3,2,1,0:T(1,128)S(1)} %get-tuple-element.14), channel_id=1, source_target_pairs={{0,2},{1,3},{4,6},{5,7},{8,10},{9,11},{12,14},{13,15},{16,18},{17,... | collective-permute-start | bytes 36872 | tf_op jit(solution)/shard_map/ppermute | solution.py:17
  70.3 5.6 %collective-permute-start.6 = (f32[1,6,1,512]{3,2,1,0:T(1,128)S(1)}, f32[1,6,1,512]{3,2,1,0:T(1,128)S(1)}, u32[]{:S(2)}, u32[]{:S(2)}) collective-permute-start(f32[1,6,1,512]{3,2,1,0:T(1,128)S(1)} %get-tuple-element.15), channel_id=1, source_target_pairs={{2,0},{3,1},{6,4},{7,5},{10,8},{11,9},{14,12},{15,13},{18,16},{19,... | collective-permute-start | bytes 36872 | tf_op jit(solution)/shard_map/ppermute | solution.py:19
  80.1 23.0 %copy-start = (f32[1,4,128,512]{3,2,1,0:T(8,128)}, f32[1,4,128,512]{3,2,1,0:T(8,128)S(1)}, u32[]{:S(2)}) copy-start(f32[1,4,128,512]{3,2,1,0:T(8,128)S(1)} %fusion.37) | copy-start | bytes 3145732
  80.2 10.2 %collective-permute-start.9 = (f32[2,1,128,512]{3,2,1,0:T(8,128)S(1)}, f32[2,1,128,512]{3,2,1,0:T(8,128)S(1)}, u32[]{:S(2)}, u32[]{:S(2)}) collective-permute-start(f32[2,1,128,512]{3,2,1,0:T(8,128)S(1)} %get-tuple-element.10), channel_id=1, source_target_pairs={{0,4},{4,8},{8,12},{1,5},{5,9},{9,13},{2,6},{6,10},{10,14},{3,7},{... | collective-permute-start | bytes 1572872 | tf_op jit(solution)/shard_map/ppermute | solution.py:17
  83.8 11.1 %collective-permute-start.8 = (f32[2,1,128,512]{3,2,1,0:T(8,128)S(1)}, f32[2,1,128,512]{3,2,1,0:T(8,128)S(1)}, u32[]{:S(2)}, u32[]{:S(2)}) collective-permute-start(f32[2,1,128,512]{3,2,1,0:T(8,128)S(1)} %get-tuple-element.11), channel_id=1, source_target_pairs={{4,0},{8,4},{12,8},{5,1},{9,5},{13,9},{6,2},{10,6},{14,10},{7,3},{... | collective-permute-start | bytes 1572872 | tf_op jit(solution)/shard_map/ppermute | solution.py:19
  94.9 3.2 %collective-permute-start.11 = (f32[2,6,1,512]{3,2,1,0:T(1,128)S(1)}, f32[2,6,1,512]{3,2,1,0:T(1,128)S(1)}, u32[]{:S(2)}, u32[]{:S(2)}) collective-permute-start(f32[2,6,1,512]{3,2,1,0:T(1,128)S(1)} %get-tuple-element.6), channel_id=1, source_target_pairs={{0,2},{1,3},{4,6},{5,7},{8,10},{9,11},{12,14},{13,15},{16,18},{17,... | collective-permute-start | bytes 73736 | tf_op jit(solution)/shard_map/ppermute | solution.py:17
  96.6 5.7 %collective-permute-start.10 = (f32[2,6,1,512]{3,2,1,0:T(1,128)S(1)}, f32[2,6,1,512]{3,2,1,0:T(1,128)S(1)}, u32[]{:S(2)}, u32[]{:S(2)}) collective-permute-start(f32[2,6,1,512]{3,2,1,0:T(1,128)S(1)} %get-tuple-element.7), channel_id=1, source_target_pairs={{2,0},{3,1},{6,4},{7,5},{10,8},{11,9},{14,12},{15,13},{18,16},{19,... | collective-permute-start | bytes 73736 | tf_op jit(solution)/shard_map/ppermute | solution.py:19
Sparse Core Ops, SparseCore 0:
  107.6 7.7 all-gather.1
